TPU v7x, 32 devices: a whole 2x2x4 slice. The times are simulated.
32 devices in a mesh: dp: 8 (over z, x), tensor: 4 (over y, core).
Axes of the slice: x: 2, y: 2, z: 4, core: 2. Of those that a mesh axis runs over, the one named last changes fastest.
Arguments:
- layer_input: bfloat16 [5120, 2304], P(('dp', 'tensor')), may hold values from -6 to 6
- cotangent: bfloat16 [5120, 2304], P(('dp', 'tensor')), may hold values from -6 to 6
- norm_gains: bfloat16 [4, 2304], replicated, may hold values from 0.25 to 1.75
- w_query: bfloat16 [2304, 2048], P('dp', 'tensor'), may hold values from -0.125 to 0.125
- w_key: bfloat16 [2304, 1024], P('dp', 'tensor'), may hold values from -0.125 to 0.125
- w_value: bfloat16 [2304, 1024], P('dp', 'tensor'), may hold values from -0.125 to 0.125
- w_output: bfloat16 [2048, 2304], P('tensor', 'dp'), may hold values from -0.125 to 0.125
- w_gate: bfloat16 [2304, 9216], P('dp', 'tensor'), may hold values from -0.125 to 0.125
- w_up: bfloat16 [2304, 9216], P('dp', 'tensor'), may hold values from -0.125 to 0.125
- w_down: bfloat16 [9216, 2304], P('tensor', 'dp'), may hold values from -0.0625 to 0.0625
- query_shrink: bfloat16 [8, 16, 2304], replicated, may hold values from -0.125 to 0.125
- key_shrink: bfloat16 [8, 16, 2304], replicated, may hold values from -0.125 to 0.125
- value_shrink: bfloat16 [8, 16, 2304], replicated, may hold values from -0.125 to 0.125
- output_shrink: bfloat16 [8, 16, 2048], P(None, None, 'tensor'), may hold values from -0.125 to 0.125
- gate_shrink: bfloat16 [8, 16, 2304], replicated, may hold values from -0.125 to 0.125
- up_shrink: bfloat16 [8, 16, 2304], replicated, may hold values from -0.125 to 0.125
- down_shrink: bfloat16 [8, 16, 9216], P(None, None, 'tensor'), may hold values from -0.0625 to 0.0625
- query_expand: bfloat16 [8, 16, 2048], P(None, None, 'tensor'), may hold values from -0.75 to 0.75
- key_expand: bfloat16 [8, 16, 1024], P(None, None, 'tensor'), may hold values from -0.75 to 0.75
- value_expand: bfloat16 [8, 16, 1024], P(None, None, 'tensor'), may hold values from -0.75 to 0.75
- output_expand: bfloat16 [8, 16, 2304], replicated, may hold values from -0.75 to 0.75
- gate_expand: bfloat16 [8, 16, 9216], P(None, None, 'tensor'), may hold values from -0.75 to 0.75
- up_expand: bfloat16 [8, 16, 9216], P(None, None, 'tensor'), may hold values from -0.75 to 0.75
- down_expand: bfloat16 [8, 16, 2304], replicated, may hold values from -0.75 to 0.75
- adapter_ids: int32 [8], P('dp'), may hold values from 0 to 7
- parent_segments: int32 [8, 13], P('dp'), may hold values from 0 to 4, as said below
- segment_ids: int32 [5120], P('dp'), may hold values from 0 to 12, as said below
Outputs:
- layer_output: bfloat16 [5120, 2304], P(('dp', 'tensor'))
- input_grad: float32 [5120, 2304], P(('dp', 'tensor'))
- shrink_query: float32 [8, 16, 2304], replicated
- shrink_key: float32 [8, 16, 2304], replicated
- shrink_value: float32 [8, 16, 2304], replicated
- shrink_output: float32 [8, 16, 2048], P(None, None, 'tensor')
- shrink_gate: float32 [8, 16, 2304], replicated
- shrink_up: float32 [8, 16, 2304], replicated
- shrink_down: float32 [8, 16, 9216], P(None, None, 'tensor')
- expand_query: float32 [8, 16, 2048], P(None, None, 'tensor')
- expand_key: float32 [8, 16, 1024], P(None, None, 'tensor')
- expand_value: float32 [8, 16, 1024], P(None, None, 'tensor')
- expand_output: float32 [8, 16, 2304], replicated
- expand_gate: float32 [8, 16, 9216], P(None, None, 'tensor')
- expand_up: float32 [8, 16, 9216], P(None, None, 'tensor')
- expand_down: float32 [8, 16, 2304], replicated
Inputs may be any that keep to these rules, and one draw needn't show every extreme that they name: `parent_segments`: in each tree, segment 0 is the trunk and is its own parent; segments 1 to 4 have parent 0; each of the other segments has a branch (1 to 4) as parent, and every branch is the parent of exactly 2 of them. `segment_ids`: the first 256 tokens of each tree are segment 0; the rest are 12 contiguous runs of 32 tokens, one run for each other segment, in any order.
All inputs are finite; a program needn't handle non-finite values.
Results may differ from a plain program's by a relative error of at most 0.028.
Values may be sent and summed in bfloat16 or wider, within the bound.
No kernel may reach another device: no remote copies, remote signals or barrier semaphores. Data moves between devices by JAX's collectives and lax.ppermute only.
A program may use at most 256 MiB of HBM per device.

v0:
```python
import math
import jax
import jax.numpy as jnp
from jax import lax
from jax.sharding import PartitionSpec as P

HEAD_WIDTH = 256
ADAPTERS = 8


def rms_scale(value_rows, gain_row):
    inverse = lax.rsqrt(jnp.mean(value_rows * value_rows, axis=-1, keepdims=True) + 1e-06)
    return value_rows * inverse * gain_row


def rms_back(value_rows, gain_row, upstream):
    inverse = lax.rsqrt(jnp.mean(value_rows * value_rows, axis=-1, keepdims=True) + 1e-06)
    scaled = gain_row * upstream
    return inverse * scaled - value_rows * (inverse * inverse * inverse) * jnp.mean(
        value_rows * scaled, axis=-1, keepdims=True
    )


def pick_from(lookup, indices, labels):
    return jnp.sum(jnp.where(indices[:, None] == labels[None, :], lookup[None, :], 0), axis=1)


def tree_tables(segments, parents):
    count_seg = parents.shape[0]
    sequence_length = segments.shape[0]
    labels = jnp.arange(count_seg, dtype=jnp.int32)
    places = jnp.arange(sequence_length, dtype=jnp.int32)
    member = segments[None, :] == labels[:, None]
    starts = jnp.min(jnp.where(member, places[None, :], sequence_length), axis=1)
    counts = jnp.sum(member.astype(jnp.int32), axis=1)
    grands = pick_from(parents, parents, labels)
    offsets = jnp.where(parents != labels, pick_from(counts, parents, labels), 0) + jnp.where(
        grands != parents, pick_from(counts, grands, labels), 0
    )
    tok_start = pick_from(starts, segments, labels)
    tok_offset = pick_from(offsets, segments, labels)
    tok_parent = pick_from(parents, segments, labels)
    tok_grand = pick_from(grands, segments, labels)
    positions = (places - tok_start + tok_offset).astype(jnp.float32)
    same_seg = (segments[None, :] == segments[:, None]) & (places[None, :] <= places[:, None])
    from_parent = (segments[None, :] == tok_parent[:, None]) & (tok_parent != segments)[:, None]
    from_grand = (segments[None, :] == tok_grand[:, None]) & (tok_grand != tok_parent)[:, None]
    visible = same_seg | from_parent | from_grand
    inv_freq = jnp.exp(
        jnp.arange(HEAD_WIDTH // 2, dtype=jnp.float32) * (-2.0 * math.log(10000.0) / HEAD_WIDTH)
    )
    angles = positions[:, None] * inv_freq[None, :]
    return (visible, jnp.cos(angles), jnp.sin(angles))


def apply_rotary(value_rows, cos_rows, sin_rows):
    half_size = value_rows.shape[-1] // 2
    front_half = value_rows[..., :half_size]
    back_half = value_rows[..., half_size:]
    return jnp.concatenate(
        [
            front_half * cos_rows - back_half * sin_rows,
            back_half * cos_rows + front_half * sin_rows,
        ],
        axis=-1,
    )


def rotate_back(value_rows, cos_rows, sin_rows):
    half_size = value_rows.shape[-1] // 2
    front_half = value_rows[..., :half_size]
    back_half = value_rows[..., half_size:]
    return jnp.concatenate(
        [
            front_half * cos_rows + back_half * sin_rows,
            back_half * cos_rows - front_half * sin_rows,
        ],
        axis=-1,
    )


def product(former, latter):
    return jnp.dot(former, latter, preferred_element_type=jnp.float32)


def select(onehot, stacked):
    return jnp.einsum("e,erc->rc", onehot, stacked, preferred_element_type=jnp.float32).astype(
        jnp.bfloat16
    )


def project(inputs, weight, shrink, expand):
    inner_rank = jnp.einsum("li,ri->lr", inputs, shrink, preferred_element_type=jnp.float32)
    return (product(inputs, weight) + product(inner_rank, expand.astype(jnp.float32)), inner_rank)


def project_back(inputs, inner_rank, upstream, weight, shrink, expand):
    grad_expand = jnp.einsum("lr,lo->ro", inner_rank, upstream, preferred_element_type=jnp.float32)
    grad_inner = jnp.einsum("lo,ro->lr", upstream, expand, preferred_element_type=jnp.float32)
    grad_shrink = jnp.einsum("lr,li->ri", grad_inner, inputs, preferred_element_type=jnp.float32)
    grad_inputs = jnp.einsum(
        "lo,io->li", upstream, weight, preferred_element_type=jnp.float32
    ) + product(grad_inner, shrink.astype(jnp.float32))
    return (grad_inputs, grad_shrink, grad_expand)


def score_block(query_rows, rotated_keys, visible):
    scores = jnp.einsum(
        "qngd,knd->ngqk", query_rows, rotated_keys, preferred_element_type=jnp.float32
    )
    bounded = jnp.tanh(scores / 50.0)
    masked = jnp.where(visible[None, None], 50.0 * bounded, -1e30)
    return (bounded, masked)


def activate(gate_in, up_in):
    return jax.nn.gelu(gate_in, approximate=True) * up_in


def on_device(
    layer_input,
    cotangent,
    norm_gains,
    w_query,
    w_key,
    w_value,
    w_output,
    w_gate,
    w_up,
    w_down,
    query_shrink,
    key_shrink,
    value_shrink,
    output_shrink,
    gate_shrink,
    up_shrink,
    down_shrink,
    query_expand,
    key_expand,
    value_expand,
    output_expand,
    gate_expand,
    up_expand,
    down_expand,
    adapter_ids,
    parent_segments,
    segment_ids,
):
    norm_gain = norm_gains.astype(jnp.float32)
    w_query, w_key, w_value, w_output, w_gate, w_up, w_down = (
        lax.all_gather(w_query, "dp", axis=0, tiled=True),
        lax.all_gather(w_key, "dp", axis=0, tiled=True),
        lax.all_gather(w_value, "dp", axis=0, tiled=True),
        lax.all_gather(w_output, "dp", axis=1, tiled=True),
        lax.all_gather(w_gate, "dp", axis=0, tiled=True),
        lax.all_gather(w_up, "dp", axis=0, tiled=True),
        lax.all_gather(w_down, "dp", axis=1, tiled=True),
    )
    labels = jnp.arange(ADAPTERS, dtype=jnp.int32)
    onehot = (labels == adapter_ids[0]).astype(jnp.bfloat16)
    chosen = [
        select(onehot, stacked)
        for stacked in (
            query_shrink,
            key_shrink,
            value_shrink,
            output_shrink,
            gate_shrink,
            up_shrink,
            down_shrink,
            query_expand,
            key_expand,
            value_expand,
            output_expand,
            gate_expand,
            up_expand,
            down_expand,
        )
    ]
    s_query, s_key, s_value, s_output, s_gate, s_up, s_down = chosen[:7]
    e_query, e_key, e_value, e_output, e_gate, e_up, e_down = chosen[7:]
    visible, cos_rows, sin_rows = tree_tables(segment_ids, parent_segments[0])
    cosine_per_head = cos_rows[:, None, :]
    sine_per_head = sin_rows[:, None, :]
    own_rows = layer_input.astype(jnp.float32)
    normed = rms_scale(own_rows, norm_gain[0]).astype(jnp.bfloat16)
    normed_all = lax.all_gather(normed, "tensor", axis=0, tiled=True)
    sequence_length = normed_all.shape[0]
    query_pre, query_inner = project(normed_all, w_query, s_query, e_query)
    key_before_rotation, key_inner = project(normed_all, w_key, s_key, e_key)
    value_projected, value_inner = project(normed_all, w_value, s_value, e_value)
    heads_q = query_pre.shape[1] // HEAD_WIDTH
    heads_kv = key_before_rotation.shape[1] // HEAD_WIDTH
    head_groups = heads_q // heads_kv
    query_rows = (
        (
            apply_rotary(
                query_pre.reshape(sequence_length, heads_q, HEAD_WIDTH),
                cosine_per_head,
                sine_per_head,
            )
            * HEAD_WIDTH ** (-0.5)
        )
        .astype(jnp.bfloat16)
        .reshape(sequence_length, heads_kv, head_groups, HEAD_WIDTH)
    )
    rotated_keys = apply_rotary(
        key_before_rotation.reshape(sequence_length, heads_kv, HEAD_WIDTH),
        cosine_per_head,
        sine_per_head,
    ).astype(jnp.bfloat16)
    value_rows = value_projected.astype(jnp.bfloat16).reshape(sequence_length, heads_kv, HEAD_WIDTH)
    bounded, masked = score_block(query_rows, rotated_keys, visible)
    row_max = jnp.max(masked, axis=-1, keepdims=True)
    exponent = jnp.exp(masked - row_max)
    row_total = jnp.sum(exponent, axis=-1, keepdims=True)
    log_total = row_max + jnp.log(row_total)
    probs_low = (exponent / row_total).astype(jnp.bfloat16)
    mixed_heads = (
        jnp.einsum("ngqk,knd->qngd", probs_low, value_rows, preferred_element_type=jnp.float32)
        .reshape(sequence_length, heads_q * HEAD_WIDTH)
        .astype(jnp.bfloat16)
    )
    attn_part, output_inner = project(mixed_heads, w_output, s_output, e_output)
    attended = lax.psum_scatter(
        attn_part.astype(jnp.bfloat16), "tensor", scatter_dimension=0, tiled=True
    ).astype(jnp.float32)
    residual = own_rows + rms_scale(attended, norm_gain[1])
    normed_ffn = rms_scale(residual, norm_gain[2]).astype(jnp.bfloat16)
    ffn_rows = lax.all_gather(normed_ffn, "tensor", axis=0, tiled=True)
    gate_pre, gate_inner = project(ffn_rows, w_gate, s_gate, e_gate)
    up_pre, up_inner = project(ffn_rows, w_up, s_up, e_up)
    hidden_full, act_back = jax.vjp(activate, gate_pre, up_pre)
    hidden = hidden_full.astype(jnp.bfloat16)
    ffn_part, down_inner = project(hidden, w_down, s_down, e_down)
    ffn_out = lax.psum_scatter(
        ffn_part.astype(jnp.bfloat16), "tensor", scatter_dimension=0, tiled=True
    ).astype(jnp.float32)
    layer_output = (residual + rms_scale(ffn_out, norm_gain[3])).astype(jnp.bfloat16)
    grad_out = cotangent.astype(jnp.float32)
    grad_ffn = rms_back(ffn_out, norm_gain[3], grad_out).astype(jnp.bfloat16)
    grad_ffn_all = lax.all_gather(grad_ffn, "tensor", axis=0, tiled=True)
    down_back = project_back(hidden, down_inner, grad_ffn_all, w_down, s_down, e_down)
    grad_gate, grad_up = act_back(down_back[0])
    grad_gate = grad_gate.astype(jnp.bfloat16)
    grad_up = grad_up.astype(jnp.bfloat16)
    gate_back = project_back(ffn_rows, gate_inner, grad_gate, w_gate, s_gate, e_gate)
    up_back = project_back(ffn_rows, up_inner, grad_up, w_up, s_up, e_up)
    grad_normed_ffn = lax.psum_scatter(
        (gate_back[0] + up_back[0]).astype(jnp.bfloat16), "tensor", scatter_dimension=0, tiled=True
    ).astype(jnp.float32)
    grad_resid = grad_out + rms_back(residual, norm_gain[2], grad_normed_ffn)
    grad_attn = rms_back(attended, norm_gain[1], grad_resid).astype(jnp.bfloat16)
    grad_attn_all = lax.all_gather(grad_attn, "tensor", axis=0, tiled=True)
    output_back = project_back(
        mixed_heads, output_inner, grad_attn_all, w_output, s_output, e_output
    )
    grad_mixed = (
        output_back[0]
        .astype(jnp.bfloat16)
        .reshape(sequence_length, heads_kv, head_groups, HEAD_WIDTH)
    )
    bounded, masked = score_block(query_rows, rotated_keys, visible)
    attn_probs = jnp.exp(masked - log_total)
    probs_low = attn_probs.astype(jnp.bfloat16)
    grad_values = (
        jnp.einsum("ngqk,qngd->knd", probs_low, grad_mixed, preferred_element_type=jnp.float32)
        .reshape(sequence_length, heads_kv * HEAD_WIDTH)
        .astype(jnp.bfloat16)
    )
    grad_probs = jnp.einsum(
        "qngd,knd->ngqk", grad_mixed, value_rows, preferred_element_type=jnp.float32
    )
    grad_capped = attn_probs * (
        grad_probs - jnp.sum(attn_probs * grad_probs, axis=-1, keepdims=True)
    )
    grad_scores = (grad_capped * (1.0 - bounded * bounded)).astype(jnp.bfloat16)
    grad_queries = jnp.einsum(
        "ngqk,knd->qngd", grad_scores, rotated_keys, preferred_element_type=jnp.float32
    ).reshape(sequence_length, heads_q, HEAD_WIDTH)
    grad_keys = jnp.einsum(
        "ngqk,qngd->knd", grad_scores, query_rows, preferred_element_type=jnp.float32
    )
    grad_qpre = (
        rotate_back(grad_queries * HEAD_WIDTH ** (-0.5), cosine_per_head, sine_per_head)
        .reshape(sequence_length, heads_q * HEAD_WIDTH)
        .astype(jnp.bfloat16)
    )
    grad_kpre = (
        rotate_back(grad_keys, cosine_per_head, sine_per_head)
        .reshape(sequence_length, heads_kv * HEAD_WIDTH)
        .astype(jnp.bfloat16)
    )
    query_back = project_back(normed_all, query_inner, grad_qpre, w_query, s_query, e_query)
    key_back = project_back(normed_all, key_inner, grad_kpre, w_key, s_key, e_key)
    value_back = project_back(normed_all, value_inner, grad_values, w_value, s_value, e_value)
    grad_normed = lax.psum_scatter(
        (query_back[0] + key_back[0] + value_back[0]).astype(jnp.bfloat16),
        "tensor",
        scatter_dimension=0,
        tiled=True,
    ).astype(jnp.float32)
    input_grad = grad_resid + rms_back(own_rows, norm_gain[0], grad_normed)
    hot_rows = onehot.astype(jnp.float32)[:, None, None]
    split_sums = (
        lax.psum((hot_rows * query_back[2][None]).astype(jnp.bfloat16), "dp").astype(jnp.float32),
        lax.psum((hot_rows * key_back[2][None]).astype(jnp.bfloat16), "dp").astype(jnp.float32),
        lax.psum((hot_rows * value_back[2][None]).astype(jnp.bfloat16), "dp").astype(jnp.float32),
        lax.psum((hot_rows * output_back[1][None]).astype(jnp.bfloat16), "dp").astype(jnp.float32),
        lax.psum((hot_rows * gate_back[2][None]).astype(jnp.bfloat16), "dp").astype(jnp.float32),
        lax.psum((hot_rows * up_back[2][None]).astype(jnp.bfloat16), "dp").astype(jnp.float32),
        lax.psum((hot_rows * down_back[1][None]).astype(jnp.bfloat16), "dp").astype(jnp.float32),
    )
    shared_sums = lax.psum(
        (
            hot_rows * query_back[1][None],
            hot_rows * key_back[1][None],
            hot_rows * value_back[1][None],
            hot_rows * output_back[2][None],
            hot_rows * gate_back[1][None],
            hot_rows * up_back[1][None],
            hot_rows * down_back[2][None],
        ),
        ("dp", "tensor"),
    )
    return (
        layer_output,
        input_grad,
        shared_sums[0],
        shared_sums[1],
        shared_sums[2],
        split_sums[3],
        shared_sums[4],
        shared_sums[5],
        split_sums[6],
        split_sums[0],
        split_sums[1],
        split_sums[2],
        shared_sums[3],
        split_sums[4],
        split_sums[5],
        shared_sums[6],
    )


def solution(mesh):
    placed = (
        P(("dp", "tensor"), None),
        P(("dp", "tensor"), None),
        P(),
        P("dp", "tensor"),
        P("dp", "tensor"),
        P("dp", "tensor"),
        P("tensor", "dp"),
        P("dp", "tensor"),
        P("dp", "tensor"),
        P("tensor", "dp"),
        P(),
        P(),
        P(),
        P(None, None, "tensor"),
        P(),
        P(),
        P(None, None, "tensor"),
        P(None, None, "tensor"),
        P(None, None, "tensor"),
        P(None, None, "tensor"),
        P(),
        P(None, None, "tensor"),
        P(None, None, "tensor"),
        P(),
        P("dp"),
        P("dp", None),
        P("dp"),
    )
    return jax.shard_map(
        on_device,
        mesh=mesh,
        in_specs=placed,
        out_specs=(
            P(("dp", "tensor"), None),
            P(("dp", "tensor"), None),
            P(),
            P(),
            P(),
            P(None, None, "tensor"),
            P(),
            P(),
            P(None, None, "tensor"),
            P(None, None, "tensor"),
            P(None, None, "tensor"),
            P(None, None, "tensor"),
            P(),
            P(None, None, "tensor"),
            P(None, None, "tensor"),
            P(),
        ),
        check_vma=False,
    )
```

profile of v0, /device:TPU:0, one launch (start us, length us, event | category | flops | bytes accessed | tf_op | source)
XLA Modules:
  0.0 1369.6 jit_solution(2153370588222020406)
XLA Ops:
  26.4 17.0 %all-gather.12.cloned.1.call-done = bf16[640,2304]{1,0:T(8,128)(2,1)} async-done(((bf16[160,2304]{1,0:T(8,128)(2,1)}), bf16[640,2304]{1,0:T(8,128)(2,1)}) %all-gather.12.cloned.1.call-update) | async-done | bytes 2949136 | tf_op jit(solution)/shard_map/all_gather | solution.py:187
  46.2 51.4 %all-gather.18.cloned.1.call-done = bf16[2304,512]{1,0:T(8,128)(2,1)} async-done(((bf16[288,512]{1,0:T(8,128)(2,1)}), bf16[2304,512]{1,0:T(8,128)(2,1)}) %all-gather.18.cloned.1.call-update) | async-done | bytes 2359312 | tf_op jit(solution)/shard_map/all_gather | solution.py:151
  109.0 30.4 %all-gather.16.cloned.1.call-done = bf16[2304,256]{1,0:T(8,128)(2,1)} async-done(((bf16[288,256]{1,0:T(8,128)(2,1)}), bf16[2304,256]{1,0:T(8,128)(2,1)}) %all-gather.16.cloned.1.call-update) | async-done | bytes 1179664 | tf_op jit(solution)/shard_map/all_gather | solution.py:152
  143.9 37.5 %all-gather.14.cloned.1.call-done = bf16[2304,256]{1,0:T(8,128)(2,1)} async-done(((bf16[288,256]{1,0:T(8,128)(2,1)}), bf16[2304,256]{1,0:T(8,128)(2,1)}) %all-gather.14.cloned.1.call-update) | async-done | bytes 1179664 | tf_op jit(solution)/shard_map/all_gather | solution.py:153
  190.3 44.0 %all-gather.20.cloned.1.call-done = bf16[512,2304]{0,1:T(8,128)(2,1)} async-done(((bf16[512,288]{0,1:T(8,128)(2,1)}), bf16[512,2304]{0,1:T(8,128)(2,1)}) %all-gather.20.cloned.1.call-update) | async-done | bytes 2359312 | tf_op jit(solution)/shard_map/all_gather | solution.py:154
  240.4 35.4 %reduce-scatter.5.cloned.1.call-done = bf16[160,2304]{1,0:T(8,128)(2,1)} async-done(((bf16[640,2304]{1,0:T(8,128)(2,1)}), bf16[160,2304]{1,0:T(8,128)(2,1)}) %reduce-scatter.5.cloned.1.call-update) | async-done | bytes 737296 | tf_op jit(solution)/shard_map/reduce_scatter | solution.py:225
  287.9 22.2 %all-gather.22.cloned.1.call-done = bf16[640,2304]{1,0:T(8,128)(2,1)} async-done(((bf16[160,2304]{1,0:T(8,128)(2,1)}), bf16[640,2304]{1,0:T(8,128)(2,1)}) %all-gather.22.cloned.1.call-update) | async-done | bytes 2949136 | tf_op jit(solution)/shard_map/all_gather | solution.py:230
  315.9 149.0 %all-gather.24.cloned.1.call-done = bf16[2304,2304]{1,0:T(8,128)(2,1)} async-done(((bf16[288,2304]{1,0:T(8,128)(2,1)}), bf16[2304,2304]{1,0:T(8,128)(2,1)}) %all-gather.24.cloned.1.call-update) | async-done | bytes 10616848 | tf_op jit(solution)/shard_map/all_gather | solution.py:155
  465.0 9.6 fusion.194
  478.0 140.1 %all-gather.26.cloned.1.call-done = bf16[2304,2304]{1,0:T(8,128)(2,1)} async-done(((bf16[288,2304]{1,0:T(8,128)(2,1)}), bf16[2304,2304]{1,0:T(8,128)(2,1)}) %all-gather.26.cloned.1.call-update) | async-done | bytes 10616848 | tf_op jit(solution)/shard_map/all_gather | solution.py:156
  618.0 9.5 fusion.195
  634.9 136.1 %all-gather.28.cloned.1.call-done = bf16[2304,2304]{0,1:T(8,128)(2,1)} async-done(((bf16[2304,288]{0,1:T(8,128)(2,1)}), bf16[2304,2304]{0,1:T(8,128)(2,1)}) %all-gather.28.cloned.1.call-update) | async-done | bytes 10616848 | tf_op jit(solution)/shard_map/all_gather | solution.py:157
  771.0 10.4 fusion.196
  784.1 35.0 %reduce-scatter.7.cloned.1.call-done = bf16[160,2304]{1,0:T(8,128)(2,1)} async-done(((bf16[640,2304]{1,0:T(8,128)(2,1)}), bf16[160,2304]{1,0:T(8,128)(2,1)}) %reduce-scatter.7.cloned.1.call-update) | async-done | bytes 737296 | tf_op jit(solution)/shard_map/reduce_scatter | solution.py:236
  823.6 27.5 %all-gather.30.cloned.1.call-done = bf16[640,2304]{1,0:T(8,128)(2,1)} async-done(((bf16[160,2304]{1,0:T(8,128)(2,1)}), bf16[640,2304]{1,0:T(8,128)(2,1)}) %all-gather.30.cloned.1.call-update) | async-done | bytes 2949136 | tf_op jit(solution)/shard_map/all_gather | solution.py:242
  851.1 11.4 fusion.197
  874.5 12.2 fusion.199
  886.7 12.2 fusion.198
  906.7 36.3 %reduce-scatter.9.cloned.1.call-done = bf16[160,2304]{1,0:T(8,128)(2,1)} async-done(((bf16[640,2304]{1,0:T(8,128)(2,1)}), bf16[160,2304]{1,0:T(8,128)(2,1)}) %reduce-scatter.9.cloned.1.call-update) | async-done | bytes 737296 | tf_op jit(solution)/shard_map/reduce_scatter | solution.py:249
  961.7 17.8 %all-gather.32.cloned.1.call-done = bf16[640,2304]{1,0:T(8,128)(2,1)} async-done(((bf16[160,2304]{1,0:T(8,128)(2,1)}), bf16[640,2304]{1,0:T(8,128)(2,1)}) %all-gather.32.cloned.1.call-update) | async-done | bytes 2949136 | tf_op jit(solution)/shard_map/all_gather | solution.py:254
  1026.7 10.2 add_convert_fusion
  1037.5 90.8 %all-reduce.7.cloned.1.call-done = (bf16[8,16,512]{2,1,0:T(8,128)(2,1)}, bf16[8,16,2304]{2,1,0:T(8,128)(2,1)}, bf16[8,16,512]{2,1,0:T(8,128)(2,1)}, bf16[8,16,25...) async-done(((bf16[8,16,512]{2,1,0:T(8,128)(2,1)}, bf16[8,16,2304]{2,1,0:T(8,128)(2,1)}, ...) | async-done | bytes 2162704 | tf_op jit(solution)/shard_map/psum | solution.py:309
  1139.2 27.3 %reduce-scatter.11.cloned.1.call-done = bf16[160,2304]{1,0:T(8,128)(2,1)} async-done(((bf16[640,2304]{1,0:T(8,128)(2,1)}), bf16[160,2304]{1,0:T(8,128)(2,1)}) %reduce-scatter.11.cloned.1.call-update) | async-done | bytes 737296 | tf_op jit(solution)/shard_map/reduce_scatter | solution.py:297
  1170.7 183.6 %all-reduce.5.cloned.1.call-done = (f32[8,16,2304]{2,1,0:T(8,128)}, f32[8,16,2304]{2,1,0:T(8,128)}, f32[8,16,2304]{2,1,0:T(8,128)}, f32[8,16,2304]{2,1,0:T(8,128...) async-done(((f32[8,16,2304]{2,1,0:T(8,128)}, f32[8,16,2304]{2,1,0:T(8,128)}, f32[8,16,2304]{2,1,0:T(8,128)}, f32[8,16,2304]{2,1,0:T(8,128)}, ...) | async-done | bytes 8257552 | tf_op jit(solution)/shard_map/psum | solution.py:314
  (446 shorter events, 196.4 us)
Async XLA Ops:
  7.3 36.1 %all-gather.12.cloned.1.call-start = ((), (), s32[]{:S(2)}) async-start(), calls=%async_computation.4 | async-start | bytes 3686400 | tf_op jit(solution)/shard_map/all_gather | solution.py:187
  10.8 269.1 %copy-start.78 = (f32[2304]{0:T(1024)}, f32[2304]{0:T(1024)S(1)}, u32[]{:S(2)}) copy-start(f32[2304]{0:T(1024)S(1)} %get-tuple-element.20) | copy-start | bytes 27652
  13.1 84.6 %all-gather.18.cloned.1.call-start = ((), (), s32[]{:S(2)}) async-start(), calls=%async_computation.7 | async-start | bytes 2654208 | tf_op jit(solution)/shard_map/all_gather | solution.py:151
  13.9 125.6 %all-gather.16.cloned.1.call-start = ((), (), s32[]{:S(2)}) async-start(), calls=%async_computation.6 | async-start | bytes 1327104 | tf_op jit(solution)/shard_map/all_gather | solution.py:152
  14.6 166.8 %all-gather.14.cloned.1.call-start = ((), (), s32[]{:S(2)}) async-start(), calls=%async_computation.5 | async-start | bytes 1327104 | tf_op jit(solution)/shard_map/all_gather | solution.py:153
  15.2 219.1 %all-gather.20.cloned.1.call-start = ((), (), s32[]{:S(2)}) async-start(), calls=%async_computation.8 | async-start | bytes 2654208 | tf_op jit(solution)/shard_map/all_gather | solution.py:154
  15.8 260.0 %reduce-scatter.5.cloned.1.call-start = ((), (), s32[]{:S(2)}) async-start(), calls=%async_computation.9 | async-start | bytes 3686400 | tf_op jit(solution)/shard_map/reduce_scatter | solution.py:225
  17.1 166.9 %copy-start.112 = (f32[640]{0:T(1024)}, f32[640]{0:T(1024)S(1)}, u32[]{:S(2)}) copy-start(f32[640]{0:T(1024)S(1)} %add_convert_fusion.5) | copy-start | bytes 7684
  22.6 120.5 %copy-start.73 = (bf16[1,16,2304]{2,0,1:T(2,128)(2,1)}, bf16[1,16,2304]{2,0,1:T(2,128)(2,1)S(1)}, u32[]{:S(2)}) copy-start(bf16[1,16,2304]{2,0,1:T(2,128)(2,1)S(1)} %fusion.92) | copy-start | bytes 221188
  24.3 164.2 %copy-start.24 = (pred[640,640]{0,1:T(8,128)(4,1)}, pred[640,640]{0,1:T(8,128)(4,1)S(1)}, u32[]{:S(2)}) copy-start(pred[640,640]{0,1:T(8,128)(4,1)S(1)} %fusion.25) | copy-start | bytes 1228804
  43.4 54.3 %copy-start.2 = (bf16[640,2304]{1,0:T(8,128)(2,1)S(1)}, bf16[640,2304]{1,0:T(8,128)(2,1)}, u32[]{:S(2)}) copy-start(bf16[640,2304]{1,0:T(8,128)(2,1)} %all-gather.12.cloned.1.call-done) | copy-start | bytes 8847364
  46.2 55.2 %copy-start.92 = (bf16[640,16]{0,1:T(8,128)(2,1)}, bf16[640,16]{0,1:T(8,128)(2,1)S(1)}, u32[]{:S(2)}) copy-start(bf16[640,16]{0,1:T(8,128)(2,1)S(1)} %fusion.129) | copy-start | bytes 61444
  190.0 47.7 %copy-start.22 = (bf16[256,2,640]{2,0,1:T(8,128)(2,1)}, bf16[256,2,640]{2,0,1:T(8,128)(2,1)S(1)}, u32[]{:S(2)}) copy-start(bf16[256,2,640]{2,0,1:T(8,128)(2,1)S(1)} %fusion.54) | copy-start | bytes 1966084
  240.4 69.7 %all-gather.22.cloned.1.call-start = ((), (), s32[]{:S(2)}) async-start(), calls=%async_computation.10 | async-start | bytes 3686400 | tf_op jit(solution)/shard_map/all_gather | solution.py:230
  282.5 182.5 %all-gather.24.cloned.1.call-start = ((), (), s32[]{:S(2)}) async-start(), calls=%async_computation.11 | async-start | bytes 11943936 | tf_op jit(solution)/shard_map/all_gather | solution.py:155
  283.3 334.8 %all-gather.26.cloned.1.call-start = ((), (), s32[]{:S(2)}) async-start(), calls=%async_computation.12 | async-start | bytes 11943936 | tf_op jit(solution)/shard_map/all_gather | solution.py:156
  284.0 487.0 %all-gather.28.cloned.1.call-start = ((), (), s32[]{:S(2)}) async-start(), calls=%async_computation.13 | async-start | bytes 11943936 | tf_op jit(solution)/shard_map/all_gather | solution.py:157
  284.6 534.6 %reduce-scatter.7.cloned.1.call-start = ((), (), s32[]{:S(2)}) async-start(), calls=%async_computation.14 | async-start | bytes 3686400 | tf_op jit(solution)/shard_map/reduce_scatter | solution.py:236
  784.1 67.1 %all-gather.30.cloned.1.call-start = ((), (), s32[]{:S(2)}) async-start(), calls=%async_computation.15 | async-start | bytes 3686400 | tf_op jit(solution)/shard_map/all_gather | solution.py:242
  823.6 119.5 %reduce-scatter.9.cloned.1.call-start = ((), (), s32[]{:S(2)}) async-start(), calls=%async_computation.16 | async-start | bytes 3686400 | tf_op jit(solution)/shard_map/reduce_scatter | solution.py:249
  906.2 73.3 %all-gather.32.cloned.1.call-start = ((), (), s32[]{:S(2)}) async-start(), calls=%async_computation.17 | async-start | bytes 3686400 | tf_op jit(solution)/shard_map/all_gather | solution.py:254
  951.9 176.5 %all-reduce.7.cloned.1.call-start = ((), (), s32[]{:S(2)}) async-start(), calls=%async_computation.20 | async-start | bytes 4325376 | tf_op jit(solution)/shard_map/psum | solution.py:309
  1021.9 144.6 %reduce-scatter.11.cloned.1.call-start = ((), (), s32[]{:S(2)}) async-start(), calls=%async_computation.18 | async-start | bytes 3686400 | tf_op jit(solution)/shard_map/reduce_scatter | solution.py:297
  1036.9 317.3 %all-reduce.5.cloned.1.call-start = ((), (), s32[]{:S(2)}) async-start(), calls=%async_computation.19 | async-start | bytes 16515072 | tf_op jit(solution)/shard_map/psum | solution.py:314
  (134 other events, 1270.1 us)
Sparse Core Ops, SparseCore 0:
  13.2 30.1 all-gather.11
  45.6 52.0 all-gather.17
  99.9 39.5 all-gather.15
  141.5 39.8 all-gather.13
  183.4 50.8 all-gather.19
  240.5 35.2 reduce-scatter.4
  282.6 27.4 all-gather.21
  312.5 152.4 all-gather.23
  467.4 150.6 all-gather.25
  620.3 150.6 all-gather.27
  784.2 34.9 reduce-scatter.6
  823.7 27.4 all-gather.29
  906.3 36.6 reduce-scatter.8
  952.0 27.4 all-gather.31
  1022.0 106.2 all-reduce.6
  1130.9 35.5 reduce-scatter.10
  1173.9 180.2 all-reduce.4
where the time goes:
time: 1380 us; the launch traced here: 1370 us
  waiting for transfers between devices  1090 us (79%)
  matrix products  187 us (14%)
  other arithmetic  55.4 us (4%)
  local copies, waits for them, and re-layouts  22.7 us (2%)
  between operations  16.2 us (1%)
    psum x1, waiting for transfers between devices, on_device(): lax.psum((hot_rows * query_back[1][None], hot_rows * key_back[1][None], h...  184 us
    all_gather x1, waiting for transfers between devices, on_device(): lax.all_gather(w_gate, 'dp', axis=0, tiled=True)  149 us
    all_gather x1, waiting for transfers between devices, on_device(): lax.all_gather(w_up, 'dp', axis=0, tiled=True)  140 us
    all_gather x1, waiting for transfers between devices, on_device(): lax.all_gather(w_down, 'dp', axis=1, tiled=True)  136 us
    psum x1, waiting for transfers between devices, on_device(): lax.psum((hot_rows * output_back[1][None]).astype(jnp.bfloat16), 'dp')  90.8 us
    dot_general x21, matrix products, product(): return jnp.dot(former, latter, preferred_element_type=jnp.float32)  83.2 us
    dot_general x7, matrix products, project_back(): jnp.einsum('lo,io->li', upstream, weight, preferred_element_type=jnp.floa...  52.5 us
    all_gather x1, waiting for transfers between devices, on_device(): lax.all_gather(w_query, 'dp', axis=0, tiled=True)  51.4 us
  transfers between devices with their start and end apart: 17, of which 17 were waited for; matrix products, arithmetic and copies ran while one was open for 8% of the time, Pallas kernels for 0%

commit v1 on v0

--- a/solution.py
+++ b/solution.py
@@ -239,7 +239,14 @@
     layer_output = (residual + rms_scale(ffn_out, norm_gain[3])).astype(jnp.bfloat16)
     grad_out = cotangent.astype(jnp.float32)
     grad_ffn = rms_back(ffn_out, norm_gain[3], grad_out).astype(jnp.bfloat16)
-    grad_ffn_all = lax.all_gather(grad_ffn, "tensor", axis=0, tiled=True)
+    ring = [grad_ffn]
+    for hop in range(3):
+        ring.append(lax.ppermute(ring[-1], "tensor", [(dev, (dev + 1) % 4) for dev in range(4)]))
+    grad_ffn_all = jnp.roll(
+        jnp.concatenate(ring[::-1], axis=0),
+        (lax.axis_index("tensor") + 1) * ring[0].shape[0],
+        axis=0,
+    )
     down_back = project_back(hidden, down_inner, grad_ffn_all, w_down, s_down, e_down)
     grad_gate, grad_up = act_back(down_back[0])
     grad_gate = grad_gate.astype(jnp.bfloat16)

time: 1380 us -> 1390 us (level)
    ppermute x0 -> x3, waiting for transfers between devices: none -> 33.1 us  [on_device(): lax.ppermute(ring[-1], 'tensor', [(dev, (dev + 1) % 4) for dev in range(4)])]
    all_gather x1 -> x0, waiting for transfers between devices: 27.5 us -> none  [on_device(): grad_ffn_all = lax.all_gather(grad_ffn, 'tensor', axis=0, tiled=True)]
  transfers between devices with their start and end apart: 17 -> 19, of which waited for: 17 -> 19; matrix products, arithmetic and copies ran while one was open for 8% -> 8% of each run, Pallas kernels for 0% -> 0%
where the time goes in v1:
time: 1390 us; the launch traced here: 1380 us
  waiting for transfers between devices  1090 us (78%)
  matrix products  189 us (14%)
  other arithmetic  54.4 us (4%)
  local copies, waits for them, and re-layouts  31.4 us (2%)
  between operations  16.5 us (1%)
    psum x1, waiting for transfers between devices, on_device(): lax.psum((hot_rows * query_back[1][None], hot_rows * key_back[1][None], h...  184 us
    all_gather x1, waiting for transfers between devices, on_device(): lax.all_gather(w_gate, 'dp', axis=0, tiled=True)  149 us
    all_gather x1, waiting for transfers between devices, on_device(): lax.all_gather(w_up, 'dp', axis=0, tiled=True)  140 us
    all_gather x1, waiting for transfers between devices, on_device(): lax.all_gather(w_down, 'dp', axis=1, tiled=True)  136 us
    psum x1, waiting for transfers between devices, on_device(): lax.psum((hot_rows * output_back[1][None]).astype(jnp.bfloat16), 'dp')  90.9 us
    dot_general x21, matrix products, product(): return jnp.dot(former, latter, preferred_element_type=jnp.float32)  78.6 us
    dot_general x7, matrix products, project_back(): jnp.einsum('lo,io->li', upstream, weight, preferred_element_type=jnp.floa...  58.7 us
    all_gather x1, waiting for transfers between devices, on_device(): lax.all_gather(w_query, 'dp', axis=0, tiled=True)  51.4 us
  transfers between devices with their start and end apart: 19, of which 19 were waited for; matrix products, arithmetic and copies ran while one was open for 8% of the time, Pallas kernels for 0%

profile of v1, /device:TPU:0, one launch (start us, length us, event | category | flops | bytes accessed | tf_op | source)
XLA Modules:
  0.0 1383.8 jit_solution(10951283702662141873)
XLA Ops:
  26.3 17.1 %all-gather.11.cloned.1.call-done = bf16[640,2304]{1,0:T(8,128)(2,1)} async-done(((bf16[160,2304]{1,0:T(8,128)(2,1)}), bf16[640,2304]{1,0:T(8,128)(2,1)}) %all-gather.11.cloned.1.call-update) | async-done | bytes 2949136 | tf_op jit(solution)/shard_map/all_gather | solution.py:187
  46.2 51.4 %all-gather.17.cloned.1.call-done = bf16[2304,512]{1,0:T(8,128)(2,1)} async-done(((bf16[288,512]{1,0:T(8,128)(2,1)}), bf16[2304,512]{1,0:T(8,128)(2,1)}) %all-gather.17.cloned.1.call-update) | async-done | bytes 2359312 | tf_op jit(solution)/shard_map/all_gather | solution.py:151
  109.0 30.5 %all-gather.15.cloned.1.call-done = bf16[2304,256]{1,0:T(8,128)(2,1)} async-done(((bf16[288,256]{1,0:T(8,128)(2,1)}), bf16[2304,256]{1,0:T(8,128)(2,1)}) %all-gather.15.cloned.1.call-update) | async-done | bytes 1179664 | tf_op jit(solution)/shard_map/all_gather | solution.py:152
  143.9 37.5 %all-gather.13.cloned.1.call-done = bf16[2304,256]{1,0:T(8,128)(2,1)} async-done(((bf16[288,256]{1,0:T(8,128)(2,1)}), bf16[2304,256]{1,0:T(8,128)(2,1)}) %all-gather.13.cloned.1.call-update) | async-done | bytes 1179664 | tf_op jit(solution)/shard_map/all_gather | solution.py:153
  190.3 44.1 %all-gather.19.cloned.1.call-done = bf16[512,2304]{0,1:T(8,128)(2,1)} async-done(((bf16[512,288]{0,1:T(8,128)(2,1)}), bf16[512,2304]{0,1:T(8,128)(2,1)}) %all-gather.19.cloned.1.call-update) | async-done | bytes 2359312 | tf_op jit(solution)/shard_map/all_gather | solution.py:154
  240.4 35.4 %reduce-scatter.5.cloned.1.call-done = bf16[160,2304]{1,0:T(8,128)(2,1)} async-done(((bf16[640,2304]{1,0:T(8,128)(2,1)}), bf16[160,2304]{1,0:T(8,128)(2,1)}) %reduce-scatter.5.cloned.1.call-update) | async-done | bytes 737296 | tf_op jit(solution)/shard_map/reduce_scatter | solution.py:225
  287.8 22.2 %all-gather.21.cloned.1.call-done = bf16[640,2304]{1,0:T(8,128)(2,1)} async-done(((bf16[160,2304]{1,0:T(8,128)(2,1)}), bf16[640,2304]{1,0:T(8,128)(2,1)}) %all-gather.21.cloned.1.call-update) | async-done | bytes 2949136 | tf_op jit(solution)/shard_map/all_gather | solution.py:230
  315.9 149.0 %all-gather.23.cloned.1.call-done = bf16[2304,2304]{1,0:T(8,128)(2,1)} async-done(((bf16[288,2304]{1,0:T(8,128)(2,1)}), bf16[2304,2304]{1,0:T(8,128)(2,1)}) %all-gather.23.cloned.1.call-update) | async-done | bytes 10616848 | tf_op jit(solution)/shard_map/all_gather | solution.py:155
  478.0 140.0 %all-gather.25.cloned.1.call-done = bf16[2304,2304]{1,0:T(8,128)(2,1)} async-done(((bf16[288,2304]{1,0:T(8,128)(2,1)}), bf16[2304,2304]{1,0:T(8,128)(2,1)}) %all-gather.25.cloned.1.call-update) | async-done | bytes 10616848 | tf_op jit(solution)/shard_map/all_gather | solution.py:156
  634.8 136.1 %all-gather.27.cloned.1.call-done = bf16[2304,2304]{0,1:T(8,128)(2,1)} async-done(((bf16[2304,288]{0,1:T(8,128)(2,1)}), bf16[2304,2304]{0,1:T(8,128)(2,1)}) %all-gather.27.cloned.1.call-update) | async-done | bytes 10616848 | tf_op jit(solution)/shard_map/all_gather | solution.py:157
  770.9 10.4 fusion.204
  783.9 35.0 %reduce-scatter.7.cloned.1.call-done = bf16[160,2304]{1,0:T(8,128)(2,1)} async-done(((bf16[640,2304]{1,0:T(8,128)(2,1)}), bf16[160,2304]{1,0:T(8,128)(2,1)}) %reduce-scatter.7.cloned.1.call-update) | async-done | bytes 737296 | tf_op jit(solution)/shard_map/reduce_scatter | solution.py:236
  823.4 10.9 collective-permute-done
  835.1 11.0 collective-permute-done.1
  846.1 11.2 collective-permute-done.2
  867.0 17.6 %fusion.6 = (bf16[640,2304]{1,0:T(8,128)(2,1)}, bf16[640,2304]{1,0:T(8,128)(2,1)S(1)}) fusion(f32[640,2304]{1,0:T(8,128)S(1)} %bitcast.326, f32[640,2304]{1,0:T(8,128)} %get-tuple-element.88, f32[640,2304]{1,0:T(8,128)} %fusion.141, bf16[2304,2304]{0,1:T(8,128)(2,1)} %all-gather.27.cloned.1.call-done, bf16[1280,2304]{1,0:T(8,128)(2,1)} %copy-done.21, ...), kind=kOutput, calls=%fused_computation.8 | convolution fusion | flops 6831636480 | bytes 37158916 | tf_op jit(solution)/shard_map/lo,io->li/dot_general | solution.py:101
  889.4 12.2 fusion.206
  901.5 12.1 fusion.205
  921.3 36.7 %reduce-scatter.9.cloned.1.call-done = bf16[160,2304]{1,0:T(8,128)(2,1)} async-done(((bf16[640,2304]{1,0:T(8,128)(2,1)}), bf16[160,2304]{1,0:T(8,128)(2,1)}) %reduce-scatter.9.cloned.1.call-update) | async-done | bytes 737296 | tf_op jit(solution)/shard_map/reduce_scatter | solution.py:256
  976.9 17.4 %all-gather.29.cloned.1.call-done = bf16[640,2304]{1,0:T(8,128)(2,1)} async-done(((bf16[160,2304]{1,0:T(8,128)(2,1)}), bf16[640,2304]{1,0:T(8,128)(2,1)}) %all-gather.29.cloned.1.call-update) | async-done | bytes 2949136 | tf_op jit(solution)/shard_map/all_gather | solution.py:261
  1040.8 10.2 add_convert_fusion
  1051.6 90.9 %all-reduce.7.cloned.1.call-done = (bf16[8,16,512]{2,1,0:T(8,128)(2,1)}, bf16[8,16,2304]{2,1,0:T(8,128)(2,1)}, bf16[8,16,512]{2,1,0:T(8,128)(2,1)}, bf16[8,16,25...) async-done(((bf16[8,16,512]{2,1,0:T(8,128)(2,1)}, bf16[8,16,2304]{2,1,0:T(8,128)(2,1)}, ...) | async-done | bytes 2162704 | tf_op jit(solution)/shard_map/psum | solution.py:316
  1153.3 27.3 %reduce-scatter.11.cloned.1.call-done = bf16[160,2304]{1,0:T(8,128)(2,1)} async-done(((bf16[640,2304]{1,0:T(8,128)(2,1)}), bf16[160,2304]{1,0:T(8,128)(2,1)}) %reduce-scatter.11.cloned.1.call-update) | async-done | bytes 737296 | tf_op jit(solution)/shard_map/reduce_scatter | solution.py:304
  1184.7 183.6 %all-reduce.5.cloned.1.call-done = (f32[8,16,2304]{2,1,0:T(8,128)}, f32[8,16,2304]{2,1,0:T(8,128)}, f32[8,16,2304]{2,1,0:T(8,128)}, f32[8,16,2304]{2,1,0:T(8,128...) async-done(((f32[8,16,2304]{2,1,0:T(8,128)}, f32[8,16,2304]{2,1,0:T(8,128)}, f32[8,16,2304]{2,1,0:T(8,128)}, f32[8,16,2304]{2,1,0:T(8,128)}, ...) | async-done | bytes 8257552 | tf_op jit(solution)/shard_map/psum | solution.py:321
  (468 shorter events, 217.8 us)
Async XLA Ops:
  7.3 36.1 %all-gather.11.cloned.1.call-start = ((), (), s32[]{:S(2)}) async-start(), calls=%async_computation.4 | async-start | bytes 3686400 | tf_op jit(solution)/shard_map/all_gather | solution.py:187
  10.8 269.1 %copy-start.85 = (f32[2304]{0:T(1024)}, f32[2304]{0:T(1024)S(1)}, u32[]{:S(2)}) copy-start(f32[2304]{0:T(1024)S(1)} %get-tuple-element.20) | copy-start | bytes 27652
  13.1 84.6 %all-gather.17.cloned.1.call-start = ((), (), s32[]{:S(2)}) async-start(), calls=%async_computation.7 | async-start | bytes 2654208 | tf_op jit(solution)/shard_map/all_gather | solution.py:151
  13.8 125.7 %all-gather.15.cloned.1.call-start = ((), (), s32[]{:S(2)}) async-start(), calls=%async_computation.6 | async-start | bytes 1327104 | tf_op jit(solution)/shard_map/all_gather | solution.py:152
  14.6 166.8 %all-gather.13.cloned.1.call-start = ((), (), s32[]{:S(2)}) async-start(), calls=%async_computation.5 | async-start | bytes 1327104 | tf_op jit(solution)/shard_map/all_gather | solution.py:153
  15.2 219.1 %all-gather.19.cloned.1.call-start = ((), (), s32[]{:S(2)}) async-start(), calls=%async_computation.8 | async-start | bytes 2654208 | tf_op jit(solution)/shard_map/all_gather | solution.py:154
  15.7 260.1 %reduce-scatter.5.cloned.1.call-start = ((), (), s32[]{:S(2)}) async-start(), calls=%async_computation.9 | async-start | bytes 3686400 | tf_op jit(solution)/shard_map/reduce_scatter | solution.py:225
  17.1 167.0 %copy-start.117 = (f32[640]{0:T(1024)}, f32[640]{0:T(1024)S(1)}, u32[]{:S(2)}) copy-start(f32[640]{0:T(1024)S(1)} %add_convert_fusion.5) | copy-start | bytes 7684
  22.5 120.5 %copy-start.79 = (bf16[1,16,2304]{2,0,1:T(2,128)(2,1)}, bf16[1,16,2304]{2,0,1:T(2,128)(2,1)S(1)}, u32[]{:S(2)}) copy-start(bf16[1,16,2304]{2,0,1:T(2,128)(2,1)S(1)} %fusion.97) | copy-start | bytes 221188
  24.2 164.3 %copy-start.26 = (pred[640,640]{0,1:T(8,128)(4,1)}, pred[640,640]{0,1:T(8,128)(4,1)S(1)}, u32[]{:S(2)}) copy-start(pred[640,640]{0,1:T(8,128)(4,1)S(1)} %fusion.30) | copy-start | bytes 1228804
  240.4 69.6 %all-gather.21.cloned.1.call-start = ((), (), s32[]{:S(2)}) async-start(), calls=%async_computation.10 | async-start | bytes 3686400 | tf_op jit(solution)/shard_map/all_gather | solution.py:230
  282.4 182.5 %all-gather.23.cloned.1.call-start = ((), (), s32[]{:S(2)}) async-start(), calls=%async_computation.11 | async-start | bytes 11943936 | tf_op jit(solution)/shard_map/all_gather | solution.py:155
  283.2 334.8 %all-gather.25.cloned.1.call-start = ((), (), s32[]{:S(2)}) async-start(), calls=%async_computation.12 | async-start | bytes 11943936 | tf_op jit(solution)/shard_map/all_gather | solution.py:156
  283.9 487.0 %all-gather.27.cloned.1.call-start = ((), (), s32[]{:S(2)}) async-start(), calls=%async_computation.13 | async-start | bytes 11943936 | tf_op jit(solution)/shard_map/all_gather | solution.py:157
  284.5 534.5 %reduce-scatter.7.cloned.1.call-start = ((), (), s32[]{:S(2)}) async-start(), calls=%async_computation.14 | async-start | bytes 3686400 | tf_op jit(solution)/shard_map/reduce_scatter | solution.py:236
  315.9 158.6 %copy-start.91 = (bf16[640,16]{0,1:T(8,128)(2,1)S(1)}, bf16[640,16]{0,1:T(8,128)(2,1)}, u32[]{:S(2)}) copy-start(bf16[640,16]{0,1:T(8,128)(2,1)} %fusion.137) | copy-start | bytes 61444
  783.9 174.1 %reduce-scatter.9.cloned.1.call-start = ((), (), s32[]{:S(2)}) async-start(), calls=%async_computation.15 | async-start | bytes 3686400 | tf_op jit(solution)/shard_map/reduce_scatter | solution.py:256
  823.4 10.9 collective-permute-start
  835.1 11.0 collective-permute-start.1
  846.1 11.2 collective-permute-start.2
  921.1 73.3 %all-gather.29.cloned.1.call-start = ((), (), s32[]{:S(2)}) async-start(), calls=%async_computation.16 | async-start | bytes 3686400 | tf_op jit(solution)/shard_map/all_gather | solution.py:261
  966.8 175.6 %all-reduce.7.cloned.1.call-start = ((), (), s32[]{:S(2)}) async-start(), calls=%async_computation.19 | async-start | bytes 4325376 | tf_op jit(solution)/shard_map/psum | solution.py:316
  1036.0 144.6 %reduce-scatter.11.cloned.1.call-start = ((), (), s32[]{:S(2)}) async-start(), calls=%async_computation.17 | async-start | bytes 3686400 | tf_op jit(solution)/shard_map/reduce_scatter | solution.py:304
  1051.0 317.3 %all-reduce.5.cloned.1.call-start = ((), (), s32[]{:S(2)}) async-start(), calls=%async_computation.18 | async-start | bytes 16515072 | tf_op jit(solution)/shard_map/psum | solution.py:321
  (141 other events, 1434.3 us)
Sparse Core Ops, SparseCore 0:
  13.2 30.1 all-gather.10
  45.5 52.0 all-gather.16
  99.8 39.6 all-gather.14
  141.5 39.8 all-gather.12
  183.4 50.8 all-gather.18
  240.5 35.2 reduce-scatter.4
  282.5 27.4 all-gather.20
  312.4 152.4 all-gather.22
  467.3 150.6 all-gather.24
  620.2 150.6 all-gather.26
  784.0 34.9 reduce-scatter.6
  921.2 36.7 reduce-scatter.8
  966.9 27.3 all-gather.28
  1036.1 106.2 all-reduce.6
  1145.0 35.5 reduce-scatter.10
  1188.0 180.2 all-reduce.4
